TPU v7x, 32 devices: a whole 2x2x4 slice. The times are simulated.
32 devices in a mesh: ctx: 8 (over z, x), head: 4 (over y, core).
Axes of the slice: x: 2, y: 2, z: 4, core: 2. Of those that a mesh axis runs over, the one named last changes fastest.
Arguments:
- hidden: bfloat16 [256, 8192], P(None, 'ctx')
- norm_gain: float32 [8192], replicated, may hold values from 0.1 to 1.9
- w_query: bfloat16 [8192, 8192], P('ctx', 'head'), may hold values from -0.0625 to 0.0625
- manifest_keys: bfloat16 [8, 4096, 128], P(None, 'ctx')
- manifest_values: bfloat16 [8, 4096, 128], P(None, 'ctx'), may hold values from -6 to 6
- w_output: bfloat16 [8192, 8192], P('head', 'ctx'), may hold values from -0.0625 to 0.0625
- valid_len: int32 [256], replicated, may hold values from 1 to 4096, as said below
- home_block: int32 [256], replicated, may hold values from 0 to 7, as said below
Outputs:
- projected: float32 [256, 8192], P('head', 'ctx')
Inputs may be any that keep to these rules, and one draw needn't show every extreme that they name: `valid_len`: every draw has a row that reads the whole manifest and a row with length 1. `home_block`: every draw assigns some row to the first block and some row to the last.
All inputs are finite; a program needn't handle non-finite values.
Results may differ from a plain program's by a relative error of at most 0.005.
The roundings to bfloat16 on the way count: a program that leaves them out, or rounds other values in their place, can miss the bound.
Values may be sent and summed in bfloat16 or wider, within the bound.
A program may use at most 128 MiB of HBM per device.

v0:
```python
import math

import jax
import jax.numpy as jnp
from jax import lax
from jax.sharding import PartitionSpec as P

H = 64
KVH = 8
HD = 128


def from_behind(block, axis, distance):
    devices = range(lax.axis_size(axis))
    route = [((i - distance) % len(devices), i) for i in devices]
    return lax.ppermute(block, axis, route)


def local_part(q_rows, row_lens, row_blocks, keys_here, values_here, ctx_index, per_kv):
    row_count = q_rows.shape[0]
    kv_local = keys_here.shape[0]
    key_span = keys_here.shape[1]
    q_four = q_rows.reshape(row_count, kv_local, per_kv, HD)
    scores = jnp.einsum("nkgd,kjd->nkgj", q_four, keys_here, preferred_element_type=jnp.float32) * (
        1.0 / math.sqrt(HD)
    )
    places = ctx_index * key_span + jnp.arange(key_span, dtype=jnp.int32)
    usable = (places[None, :] < row_lens[:, None]) | (row_blocks[:, None] == ctx_index)
    usable_four = usable[:, None, None, :]
    scores = jnp.where(usable_four, scores, -1e30)
    row_max = jnp.max(scores, axis=3)
    expo_vals = jnp.where(usable_four, jnp.exp(scores - row_max[..., None]), 0.0)
    row_sum = jnp.sum(expo_vals, axis=3)
    weighted = jnp.einsum(
        "nkgj,kjd->nkgd",
        expo_vals.astype(jnp.bfloat16),
        values_here,
        preferred_element_type=jnp.float32,
    )
    heads_here = kv_local * per_kv
    return (
        row_max.reshape(row_count, heads_here),
        row_sum.reshape(row_count, heads_here),
        weighted.reshape(row_count, heads_here * HD),
    )


def combine_states(first, second):
    new_max = jnp.maximum(first[0], second[0])
    first_wt = jnp.exp(first[0] - new_max)
    second_wt = jnp.exp(second[0] - new_max)
    new_sum = first_wt * first[1] + second_wt * second[1]
    new_out = (
        jnp.repeat(first_wt, HD, axis=1) * first[2] + jnp.repeat(second_wt, HD, axis=1) * second[2]
    )
    return (new_max, new_sum, new_out)


def shards(
    hidden, norm_gain, w_query, manifest_keys, manifest_values, w_output, valid_len, home_block
):
    ctx_count = lax.axis_size("ctx")
    ctx_index = lax.axis_index("ctx")
    head_index = lax.axis_index("head")
    width = w_query.shape[1]
    heads_here = width // HD
    group_size = H // KVH
    kv_local = max(1, heads_here // group_size)
    per_kv = heads_here // kv_local
    all_rows = hidden.shape[0]
    rows_dev = all_rows // ctx_count
    kv_start = head_index * heads_here // group_size
    keys_here = lax.dynamic_slice_in_dim(manifest_keys, kv_start, kv_local, 0)
    values_here = lax.dynamic_slice_in_dim(manifest_values, kv_start, kv_local, 0)
    rows_in = lax.all_to_all(hidden, "ctx", split_axis=0, concat_axis=1, tiled=True)
    widened = rows_in.astype(jnp.float32)
    inv_rms = lax.rsqrt(jnp.mean(widened * widened, axis=1, keepdims=True) + 1e-05)
    normed = (widened * inv_rms * norm_gain[None, :]).astype(jnp.bfloat16)
    query = jnp.dot(
        normed,
        lax.all_gather(w_query, "ctx", axis=0, tiled=True),
        preferred_element_type=jnp.float32,
    ).astype(jnp.bfloat16)

    def attend(q_rows, first_row):
        row_count = q_rows.shape[0]
        row_lens = lax.dynamic_slice_in_dim(valid_len, first_row, row_count, 0)
        row_blocks = lax.dynamic_slice_in_dim(home_block, first_row, row_count, 0)
        return local_part(q_rows, row_lens, row_blocks, keys_here, values_here, ctx_index, per_kv)

    def visit(hop_index, carry):
        q_current = carry[0]
        owner = (ctx_index - hop_index) % ctx_count
        state = combine_states((carry[1], carry[2], carry[3]), attend(q_current, owner * rows_dev))
        q_next = from_behind(q_current, "ctx", 1)
        moved = from_behind((state[0], state[1], state[2]), "ctx", 1)
        return (q_next, moved[0], moved[1], moved[2])

    start_state = (
        query,
        jnp.full((rows_dev, heads_here), -1e30, jnp.float32),
        jnp.zeros((rows_dev, heads_here), jnp.float32),
        jnp.zeros((rows_dev, width), jnp.float32),
    )
    final_carry = lax.fori_loop(0, ctx_count - 1, visit, start_state)
    owner = (ctx_index + 1) % ctx_count
    max_run, sum_run, out_run = combine_states(
        (final_carry[1], final_carry[2], final_carry[3]), attend(final_carry[0], owner * rows_dev)
    )
    normalized = (
        (out_run.reshape(rows_dev, heads_here, HD) / sum_run[..., None])
        .reshape(rows_dev, width)
        .astype(jnp.bfloat16)
    )
    gathered = lax.all_gather(normalized, "ctx", axis=0, tiled=True)
    gathered = jnp.roll(gathered, rows_dev, axis=0)
    return lax.psum_scatter(
        jnp.dot(gathered, w_output, preferred_element_type=jnp.float32),
        "head",
        scatter_dimension=0,
        tiled=True,
    )


def solution(mesh):
    in_specs = (
        P(None, "ctx"),
        P(),
        P("ctx", "head"),
        P(None, "ctx", None),
        P(None, "ctx", None),
        P("head", "ctx"),
        P(),
        P(),
    )
    out_specs = P("head", "ctx")
    return jax.shard_map(shards, mesh=mesh, in_specs=in_specs, out_specs=out_specs, check_vma=False)
```

profile of v0, /device:TPU:1, one launch (start us, length us, event | category | flops | bytes accessed | tf_op | source)
XLA Modules:
  0.0 842.3 jit_solution(14282002996194584548)
XLA Ops:
  6.5 0.7 all-gather.3.cloned.1.call-update
  7.3 6.4 all-to-all-start
  13.9 1.1 constant_dynamic-slice_fusion
  15.0 12.7 %all-to-all-done = bf16[8,32,1024]{2,1,0:T(8,128)(2,1)S(1)} async-done(((bf16[8,32,1024]{2,1,0:T(8,128)(2,1)}), bf16[8,32,1024]{2,1,0:T(8,128)(2,1)S(1)}, u32[]{:S(2)}, u32[]{:S(2)}) %all-to-all-start) | async-done | bytes 524320 | tf_op jit(solution)/shard_map/all_to_all | solution.py:75
  28.2 624.4 %all-gather.3.cloned.1.call-done = bf16[8192,2048]{1,0:T(8,128)(2,1)} async-done(((bf16[1024,2048]{1,0:T(8,128)(2,1)}), bf16[8192,2048]{1,0:T(8,128)(2,1)}) %all-gather.3.cloned.1.call-update) | async-done | bytes 33554448 | tf_op jit(solution)/shard_map/all_gather | solution.py:81
  652.6 13.6 %convolution_convert_fusion = bf16[32,2048]{1,0:T(8,128)(2,1)S(1)} fusion(bf16[8192,2048]{1,0:T(8,128)(2,1)} %all-gather.3.cloned.1.call-done, f32[32,8192]{1,0:T(8,128)S(1)} %bitcast.138, f32[8192]{0:T(1024)S(1)} %copy-done, f32[32]{0:T(128)S(1)} %add_rsqrt_fusion), kind=kOutput, calls=%fused_computation.23 | convolution fusion | flops 1074593792 | bytes 34766976 | tf_op jit(solution)/shard_map/dot_general | solution.py:79
  666.3 91.7 %while.21 = (s32[]{:T(128)}, bf16[32,2048]{1,0:T(8,128)(2,1)S(1)}, f32[32,16]{0,1:T(8,128)S(1)}, f32[32,16]{0,1:T(8,128)S(1)}, f32[32,2048]{1,0:T(8,128)S(1)}, /...) while((s32[]{:T(128)}, bf16[32,2048]{1,0:T(8,128)(2,1)S(1)}, ...), condition=%wide.region_4.5_spmd, body=%wide.region_1.4_spmd.sunk | while | flops 136284720 | bytes 8625204 | solution.py:105
  666.6 0.4 fusion.51
  667.0 0.4 fusion.52
  667.4 0.4 convolution_bitcast_fusion.3
  668.6 2.4 collective-permute-start
  671.0 1.5 collective-permute-start.2
  672.5 9.1 %collective-permute-done.1 = f32[32,16]{0,1:T(8,128)S(1)} collective-permute-done((f32[32,16]{0,1:T(8,128)S(1)}, f32[32,16]{0,1:T(8,128)S(1)}, u32[]{:S(2)}, u32[]{:S(2)}) %collective-permute-start.1) | collective-permute-done | bytes 2080 | tf_op jit(solution)/shard_map/while/body/eval_jaxpr/ppermute | solution.py:16
  682.1 0.4 fusion.51
  682.5 0.4 fusion.52
  682.9 0.4 convolution_bitcast_fusion.3
  684.1 0.6 collective-permute-start
  684.7 1.4 collective-permute-start.2
  686.2 10.1 %collective-permute-done.1 = f32[32,16]{0,1:T(8,128)S(1)} collective-permute-done((f32[32,16]{0,1:T(8,128)S(1)}, f32[32,16]{0,1:T(8,128)S(1)}, u32[]{:S(2)}, u32[]{:S(2)}) %collective-permute-start.1) | collective-permute-done | bytes 2080 | tf_op jit(solution)/shard_map/while/body/eval_jaxpr/ppermute | solution.py:16
  696.7 0.4 fusion.51
  697.1 0.4 fusion.52
  697.5 0.4 convolution_bitcast_fusion.3
  698.9 11.0 %collective-permute-done.1 = f32[32,16]{0,1:T(8,128)S(1)} collective-permute-done((f32[32,16]{0,1:T(8,128)S(1)}, f32[32,16]{0,1:T(8,128)S(1)}, u32[]{:S(2)}, u32[]{:S(2)}) %collective-permute-start.1) | collective-permute-done | bytes 2080 | tf_op jit(solution)/shard_map/while/body/eval_jaxpr/ppermute | solution.py:16
  710.4 0.4 fusion.51
  710.8 0.4 fusion.52
  711.1 0.4 convolution_bitcast_fusion.3
  712.5 10.1 %collective-permute-done.1 = f32[32,16]{0,1:T(8,128)S(1)} collective-permute-done((f32[32,16]{0,1:T(8,128)S(1)}, f32[32,16]{0,1:T(8,128)S(1)}, u32[]{:S(2)}, u32[]{:S(2)}) %collective-permute-start.1) | collective-permute-done | bytes 2080 | tf_op jit(solution)/shard_map/while/body/eval_jaxpr/ppermute | solution.py:16
  723.1 0.4 fusion.51
  723.5 0.4 fusion.52
  723.9 0.4 convolution_bitcast_fusion.3
  725.3 9.2 %collective-permute-done.1 = f32[32,16]{0,1:T(8,128)S(1)} collective-permute-done((f32[32,16]{0,1:T(8,128)S(1)}, f32[32,16]{0,1:T(8,128)S(1)}, u32[]{:S(2)}, u32[]{:S(2)}) %collective-permute-start.1) | collective-permute-done | bytes 2080 | tf_op jit(solution)/shard_map/while/body/eval_jaxpr/ppermute | solution.py:16
  734.9 0.4 fusion.51
  735.2 0.4 fusion.52
  735.6 0.4 convolution_bitcast_fusion.3
  737.0 9.2 %collective-permute-done.1 = f32[32,16]{0,1:T(8,128)S(1)} collective-permute-done((f32[32,16]{0,1:T(8,128)S(1)}, f32[32,16]{0,1:T(8,128)S(1)}, u32[]{:S(2)}, u32[]{:S(2)}) %collective-permute-start.1) | collective-permute-done | bytes 2080 | tf_op jit(solution)/shard_map/while/body/eval_jaxpr/ppermute | solution.py:16
  746.6 0.4 fusion.51
  747.0 0.4 fusion.52
  747.3 0.4 convolution_bitcast_fusion.3
  748.7 9.2 %collective-permute-done.1 = f32[32,16]{0,1:T(8,128)S(1)} collective-permute-done((f32[32,16]{0,1:T(8,128)S(1)}, f32[32,16]{0,1:T(8,128)S(1)}, u32[]{:S(2)}, u32[]{:S(2)}) %collective-permute-start.1) | collective-permute-done | bytes 2080 | tf_op jit(solution)/shard_map/while/body/eval_jaxpr/ppermute | solution.py:16
  758.1 0.4 fusion.40
  758.4 0.4 convolution_bitcast_fusion.1
  758.8 0.3 fusion.18
  760.0 1.0 fusion.26
  761.0 43.4 %all-gather.5.cloned.1.call-done = bf16[256,2048]{1,0:T(8,128)(2,1)} async-done(((bf16[32,2048]{1,0:T(8,128)(2,1)}), bf16[256,2048]{1,0:T(8,128)(2,1)}) %all-gather.5.cloned.1.call-update) | async-done | bytes 1048592 | tf_op jit(solution)/shard_map/all_gather | solution.py:115
  804.4 1.2 slice.11
  805.6 0.9 slice.10
  806.5 4.4 fusion.14
  811.0 24.8 %reduce-scatter.2.cloned.1.call-done = f32[64,1024]{1,0:T(8,128)} async-done(((f32[256,1024]{1,0:T(8,128)}), f32[64,1024]{1,0:T(8,128)}) %reduce-scatter.2.cloned.1.call-update) | async-done | bytes 262160 | tf_op jit(solution)/shard_map/reduce_scatter | solution.py:117
  (167 shorter events, 10.8 us)
Async XLA Ops:
  6.5 7.2 copy-start.2
  6.5 7.3 copy-start.1
  6.5 646.1 %all-gather.3.cloned.1.call-start = ((), (), s32[]{:S(2)}) async-start(), calls=%async_computation.2 | async-start | bytes 37748736 | tf_op jit(solution)/shard_map/all_gather | solution.py:81
  7.3 645.3 %copy-start = (f32[8192]{0:T(1024)S(1)}, f32[8192]{0:T(1024)}, u32[]{:S(2)}) copy-start(f32[8192]{0:T(1024)} %param.11) | copy-start | bytes 98308
  7.3 20.4 %all-to-all-start = ((bf16[8,32,1024]{2,1,0:T(8,128)(2,1)}), bf16[8,32,1024]{2,1,0:T(8,128)(2,1)S(1)}, u32[]{:S(2)}, u32[]{:S(2)}) async-start(bf16[8,32,1024]{2,1,0:T(8,128)(2,1)} %bitcast.8), calls=%async_computation | async-start | bytes 1048576 | tf_op jit(solution)/shard_map/all_to_all | solution.py:75
  13.6 790.7 %all-gather.5.cloned.1.call-start = ((), (), s32[]{:S(2)}) async-start(), calls=%async_computation.3 | async-start | bytes 1179648 | tf_op jit(solution)/shard_map/all_gather | solution.py:115
  668.5 13.3 %collective-permute-start.3 = (f32[32,2048]{1,0:T(8,128)S(1)}, f32[32,2048]{1,0:T(8,128)S(1)}, u32[]{:S(2)}, u32[]{:S(2)}) collective-permute-start(f32[32,2048]{1,0:T(8,128)S(1)} %fusion.54), channel_id=1, source_target_pairs={{28,0},{0,4},{4,8},{8,12},{12,16},{16,20},{20,24},{24,28},{29,1},{... | collective-permute-start | bytes 786440 | tf_op jit(solution)/shard_map/while/body/eval_jaxpr/ppermute | solution.py:16
  668.6 13.3 %collective-permute-start = (bf16[32,2048]{1,0:T(8,128)(2,1)S(1)}, bf16[32,2048]{1,0:T(8,128)(2,1)S(1)}, u32[]{:S(2)}, u32[]{:S(2)}) collective-permute-start(bf16[32,2048]{1,0:T(8,128)(2,1)S(1)} %copy.94), channel_id=1, source_target_pairs={{28,0},{0,4},{4,8},{8,12},{12,16},{16,20},{20,24},{24,28},{29,1},{... | collective-permute-start | bytes 393224 | tf_op jit(solution)/shard_map/while/body/eval_jaxpr/ppermute | solution.py:16
  670.9 10.7 %collective-permute-start.1 = (f32[32,16]{0,1:T(8,128)S(1)}, f32[32,16]{0,1:T(8,128)S(1)}, u32[]{:S(2)}, u32[]{:S(2)}) collective-permute-start(f32[32,16]{0,1:T(8,128)S(1)} %get-tuple-element.376), channel_id=1, source_target_pairs={{28,0},{0,4},{4,8},{8,12},{12,16},{16,20},{20,24},{24,28},{29,1},{... | collective-permute-start | bytes 6152 | tf_op jit(solution)/shard_map/while/body/eval_jaxpr/ppermute | solution.py:16
  671.0 10.8 %collective-permute-start.2 = (f32[32,16]{0,1:T(8,128)S(1)}, f32[32,16]{0,1:T(8,128)S(1)}, u32[]{:S(2)}, u32[]{:S(2)}) collective-permute-start(f32[32,16]{0,1:T(8,128)S(1)} %get-tuple-element.377), channel_id=1, source_target_pairs={{28,0},{0,4},{4,8},{8,12},{12,16},{16,20},{20,24},{24,28},{29,1},{... | collective-permute-start | bytes 6152 | tf_op jit(solution)/shard_map/while/body/eval_jaxpr/ppermute | solution.py:16
  684.0 12.4 %collective-permute-start.3 = (f32[32,2048]{1,0:T(8,128)S(1)}, f32[32,2048]{1,0:T(8,128)S(1)}, u32[]{:S(2)}, u32[]{:S(2)}) collective-permute-start(f32[32,2048]{1,0:T(8,128)S(1)} %fusion.54), channel_id=1, source_target_pairs={{28,0},{0,4},{4,8},{8,12},{12,16},{16,20},{20,24},{24,28},{29,1},{... | collective-permute-start | bytes 786440 | tf_op jit(solution)/shard_map/while/body/eval_jaxpr/ppermute | solution.py:16
  684.1 12.4 %collective-permute-start = (bf16[32,2048]{1,0:T(8,128)(2,1)S(1)}, bf16[32,2048]{1,0:T(8,128)(2,1)S(1)}, u32[]{:S(2)}, u32[]{:S(2)}) collective-permute-start(bf16[32,2048]{1,0:T(8,128)(2,1)S(1)} %copy.94), channel_id=1, source_target_pairs={{28,0},{0,4},{4,8},{8,12},{12,16},{16,20},{20,24},{24,28},{29,1},{... | collective-permute-start | bytes 393224 | tf_op jit(solution)/shard_map/while/body/eval_jaxpr/ppermute | solution.py:16
  684.6 11.6 %collective-permute-start.1 = (f32[32,16]{0,1:T(8,128)S(1)}, f32[32,16]{0,1:T(8,128)S(1)}, u32[]{:S(2)}, u32[]{:S(2)}) collective-permute-start(f32[32,16]{0,1:T(8,128)S(1)} %get-tuple-element.376), channel_id=1, source_target_pairs={{28,0},{0,4},{4,8},{8,12},{12,16},{16,20},{20,24},{24,28},{29,1},{... | collective-permute-start | bytes 6152 | tf_op jit(solution)/shard_map/while/body/eval_jaxpr/ppermute | solution.py:16
  684.7 11.7 %collective-permute-start.2 = (f32[32,16]{0,1:T(8,128)S(1)}, f32[32,16]{0,1:T(8,128)S(1)}, u32[]{:S(2)}, u32[]{:S(2)}) collective-permute-start(f32[32,16]{0,1:T(8,128)S(1)} %get-tuple-element.377), channel_id=1, source_target_pairs={{28,0},{0,4},{4,8},{8,12},{12,16},{16,20},{20,24},{24,28},{29,1},{... | collective-permute-start | bytes 6152 | tf_op jit(solution)/shard_map/while/body/eval_jaxpr/ppermute | solution.py:16
  698.6 11.5 %collective-permute-start.3 = (f32[32,2048]{1,0:T(8,128)S(1)}, f32[32,2048]{1,0:T(8,128)S(1)}, u32[]{:S(2)}, u32[]{:S(2)}) collective-permute-start(f32[32,2048]{1,0:T(8,128)S(1)} %fusion.54), channel_id=1, source_target_pairs={{28,0},{0,4},{4,8},{8,12},{12,16},{16,20},{20,24},{24,28},{29,1},{... | collective-permute-start | bytes 786440 | tf_op jit(solution)/shard_map/while/body/eval_jaxpr/ppermute | solution.py:16
  698.7 11.4 %collective-permute-start = (bf16[32,2048]{1,0:T(8,128)(2,1)S(1)}, bf16[32,2048]{1,0:T(8,128)(2,1)S(1)}, u32[]{:S(2)}, u32[]{:S(2)}) collective-permute-start(bf16[32,2048]{1,0:T(8,128)(2,1)S(1)} %copy.94), channel_id=1, source_target_pairs={{28,0},{0,4},{4,8},{8,12},{12,16},{16,20},{20,24},{24,28},{29,1},{... | collective-permute-start | bytes 393224 | tf_op jit(solution)/shard_map/while/body/eval_jaxpr/ppermute | solution.py:16
  698.7 11.2 %collective-permute-start.1 = (f32[32,16]{0,1:T(8,128)S(1)}, f32[32,16]{0,1:T(8,128)S(1)}, u32[]{:S(2)}, u32[]{:S(2)}) collective-permute-start(f32[32,16]{0,1:T(8,128)S(1)} %get-tuple-element.376), channel_id=1, source_target_pairs={{28,0},{0,4},{4,8},{8,12},{12,16},{16,20},{20,24},{24,28},{29,1},{... | collective-permute-start | bytes 6152 | tf_op jit(solution)/shard_map/while/body/eval_jaxpr/ppermute | solution.py:16
  698.8 11.3 %collective-permute-start.2 = (f32[32,16]{0,1:T(8,128)S(1)}, f32[32,16]{0,1:T(8,128)S(1)}, u32[]{:S(2)}, u32[]{:S(2)}) collective-permute-start(f32[32,16]{0,1:T(8,128)S(1)} %get-tuple-element.377), channel_id=1, source_target_pairs={{28,0},{0,4},{4,8},{8,12},{12,16},{16,20},{20,24},{24,28},{29,1},{... | collective-permute-start | bytes 6152 | tf_op jit(solution)/shard_map/while/body/eval_jaxpr/ppermute | solution.py:16
  712.3 10.6 %collective-permute-start.3 = (f32[32,2048]{1,0:T(8,128)S(1)}, f32[32,2048]{1,0:T(8,128)S(1)}, u32[]{:S(2)}, u32[]{:S(2)}) collective-permute-start(f32[32,2048]{1,0:T(8,128)S(1)} %fusion.54), channel_id=1, source_target_pairs={{28,0},{0,4},{4,8},{8,12},{12,16},{16,20},{20,24},{24,28},{29,1},{... | collective-permute-start | bytes 786440 | tf_op jit(solution)/shard_map/while/body/eval_jaxpr/ppermute | solution.py:16
  712.3 10.5 %collective-permute-start = (bf16[32,2048]{1,0:T(8,128)(2,1)S(1)}, bf16[32,2048]{1,0:T(8,128)(2,1)S(1)}, u32[]{:S(2)}, u32[]{:S(2)}) collective-permute-start(bf16[32,2048]{1,0:T(8,128)(2,1)S(1)} %copy.94), channel_id=1, source_target_pairs={{28,0},{0,4},{4,8},{8,12},{12,16},{16,20},{20,24},{24,28},{29,1},{... | collective-permute-start | bytes 393224 | tf_op jit(solution)/shard_map/while/body/eval_jaxpr/ppermute | solution.py:16
  712.4 10.3 %collective-permute-start.1 = (f32[32,16]{0,1:T(8,128)S(1)}, f32[32,16]{0,1:T(8,128)S(1)}, u32[]{:S(2)}, u32[]{:S(2)}) collective-permute-start(f32[32,16]{0,1:T(8,128)S(1)} %get-tuple-element.376), channel_id=1, source_target_pairs={{28,0},{0,4},{4,8},{8,12},{12,16},{16,20},{20,24},{24,28},{29,1},{... | collective-permute-start | bytes 6152 | tf_op jit(solution)/shard_map/while/body/eval_jaxpr/ppermute | solution.py:16
  712.5 10.4 %collective-permute-start.2 = (f32[32,16]{0,1:T(8,128)S(1)}, f32[32,16]{0,1:T(8,128)S(1)}, u32[]{:S(2)}, u32[]{:S(2)}) collective-permute-start(f32[32,16]{0,1:T(8,128)S(1)} %get-tuple-element.377), channel_id=1, source_target_pairs={{28,0},{0,4},{4,8},{8,12},{12,16},{16,20},{20,24},{24,28},{29,1},{... | collective-permute-start | bytes 6152 | tf_op jit(solution)/shard_map/while/body/eval_jaxpr/ppermute | solution.py:16
  725.0 9.6 %collective-permute-start.3 = (f32[32,2048]{1,0:T(8,128)S(1)}, f32[32,2048]{1,0:T(8,128)S(1)}, u32[]{:S(2)}, u32[]{:S(2)}) collective-permute-start(f32[32,2048]{1,0:T(8,128)S(1)} %fusion.54), channel_id=1, source_target_pairs={{28,0},{0,4},{4,8},{8,12},{12,16},{16,20},{20,24},{24,28},{29,1},{... | collective-permute-start | bytes 786440 | tf_op jit(solution)/shard_map/while/body/eval_jaxpr/ppermute | solution.py:16
  725.1 9.5 %collective-permute-start = (bf16[32,2048]{1,0:T(8,128)(2,1)S(1)}, bf16[32,2048]{1,0:T(8,128)(2,1)S(1)}, u32[]{:S(2)}, u32[]{:S(2)}) collective-permute-start(bf16[32,2048]{1,0:T(8,128)(2,1)S(1)} %copy.94), channel_id=1, source_target_pairs={{28,0},{0,4},{4,8},{8,12},{12,16},{16,20},{20,24},{24,28},{29,1},{... | collective-permute-start | bytes 393224 | tf_op jit(solution)/shard_map/while/body/eval_jaxpr/ppermute | solution.py:16
  725.1 9.3 %collective-permute-start.1 = (f32[32,16]{0,1:T(8,128)S(1)}, f32[32,16]{0,1:T(8,128)S(1)}, u32[]{:S(2)}, u32[]{:S(2)}) collective-permute-start(f32[32,16]{0,1:T(8,128)S(1)} %get-tuple-element.376), channel_id=1, source_target_pairs={{28,0},{0,4},{4,8},{8,12},{12,16},{16,20},{20,24},{24,28},{29,1},{... | collective-permute-start | bytes 6152 | tf_op jit(solution)/shard_map/while/body/eval_jaxpr/ppermute | solution.py:16
  725.2 9.4 %collective-permute-start.2 = (f32[32,16]{0,1:T(8,128)S(1)}, f32[32,16]{0,1:T(8,128)S(1)}, u32[]{:S(2)}, u32[]{:S(2)}) collective-permute-start(f32[32,16]{0,1:T(8,128)S(1)} %get-tuple-element.377), channel_id=1, source_target_pairs={{28,0},{0,4},{4,8},{8,12},{12,16},{16,20},{20,24},{24,28},{29,1},{... | collective-permute-start | bytes 6152 | tf_op jit(solution)/shard_map/while/body/eval_jaxpr/ppermute | solution.py:16
  736.7 9.6 %collective-permute-start.3 = (f32[32,2048]{1,0:T(8,128)S(1)}, f32[32,2048]{1,0:T(8,128)S(1)}, u32[]{:S(2)}, u32[]{:S(2)}) collective-permute-start(f32[32,2048]{1,0:T(8,128)S(1)} %fusion.54), channel_id=1, source_target_pairs={{28,0},{0,4},{4,8},{8,12},{12,16},{16,20},{20,24},{24,28},{29,1},{... | collective-permute-start | bytes 786440 | tf_op jit(solution)/shard_map/while/body/eval_jaxpr/ppermute | solution.py:16
  736.8 9.5 %collective-permute-start = (bf16[32,2048]{1,0:T(8,128)(2,1)S(1)}, bf16[32,2048]{1,0:T(8,128)(2,1)S(1)}, u32[]{:S(2)}, u32[]{:S(2)}) collective-permute-start(bf16[32,2048]{1,0:T(8,128)(2,1)S(1)} %copy.94), channel_id=1, source_target_pairs={{28,0},{0,4},{4,8},{8,12},{12,16},{16,20},{20,24},{24,28},{29,1},{... | collective-permute-start | bytes 393224 | tf_op jit(solution)/shard_map/while/body/eval_jaxpr/ppermute | solution.py:16
  736.9 9.3 %collective-permute-start.1 = (f32[32,16]{0,1:T(8,128)S(1)}, f32[32,16]{0,1:T(8,128)S(1)}, u32[]{:S(2)}, u32[]{:S(2)}) collective-permute-start(f32[32,16]{0,1:T(8,128)S(1)} %get-tuple-element.376), channel_id=1, source_target_pairs={{28,0},{0,4},{4,8},{8,12},{12,16},{16,20},{20,24},{24,28},{29,1},{... | collective-permute-start | bytes 6152 | tf_op jit(solution)/shard_map/while/body/eval_jaxpr/ppermute | solution.py:16
  736.9 9.4 %collective-permute-start.2 = (f32[32,16]{0,1:T(8,128)S(1)}, f32[32,16]{0,1:T(8,128)S(1)}, u32[]{:S(2)}, u32[]{:S(2)}) collective-permute-start(f32[32,16]{0,1:T(8,128)S(1)} %get-tuple-element.377), channel_id=1, source_target_pairs={{28,0},{0,4},{4,8},{8,12},{12,16},{16,20},{20,24},{24,28},{29,1},{... | collective-permute-start | bytes 6152 | tf_op jit(solution)/shard_map/while/body/eval_jaxpr/ppermute | solution.py:16
  748.5 9.6 %collective-permute-start.3 = (f32[32,2048]{1,0:T(8,128)S(1)}, f32[32,2048]{1,0:T(8,128)S(1)}, u32[]{:S(2)}, u32[]{:S(2)}) collective-permute-start(f32[32,2048]{1,0:T(8,128)S(1)} %fusion.54), channel_id=1, source_target_pairs={{28,0},{0,4},{4,8},{8,12},{12,16},{16,20},{20,24},{24,28},{29,1},{... | collective-permute-start | bytes 786440 | tf_op jit(solution)/shard_map/while/body/eval_jaxpr/ppermute | solution.py:16
  748.5 9.5 %collective-permute-start = (bf16[32,2048]{1,0:T(8,128)(2,1)S(1)}, bf16[32,2048]{1,0:T(8,128)(2,1)S(1)}, u32[]{:S(2)}, u32[]{:S(2)}) collective-permute-start(bf16[32,2048]{1,0:T(8,128)(2,1)S(1)} %copy.94), channel_id=1, source_target_pairs={{28,0},{0,4},{4,8},{8,12},{12,16},{16,20},{20,24},{24,28},{29,1},{... | collective-permute-start | bytes 393224 | tf_op jit(solution)/shard_map/while/body/eval_jaxpr/ppermute | solution.py:16
  748.6 9.3 %collective-permute-start.1 = (f32[32,16]{0,1:T(8,128)S(1)}, f32[32,16]{0,1:T(8,128)S(1)}, u32[]{:S(2)}, u32[]{:S(2)}) collective-permute-start(f32[32,16]{0,1:T(8,128)S(1)} %get-tuple-element.376), channel_id=1, source_target_pairs={{28,0},{0,4},{4,8},{8,12},{12,16},{16,20},{20,24},{24,28},{29,1},{... | collective-permute-start | bytes 6152 | tf_op jit(solution)/shard_map/while/body/eval_jaxpr/ppermute | solution.py:16
  748.7 9.4 %collective-permute-start.2 = (f32[32,16]{0,1:T(8,128)S(1)}, f32[32,16]{0,1:T(8,128)S(1)}, u32[]{:S(2)}, u32[]{:S(2)}) collective-permute-start(f32[32,16]{0,1:T(8,128)S(1)} %get-tuple-element.377), channel_id=1, source_target_pairs={{28,0},{0,4},{4,8},{8,12},{12,16},{16,20},{20,24},{24,28},{29,1},{... | collective-permute-start | bytes 6152 | tf_op jit(solution)/shard_map/while/body/eval_jaxpr/ppermute | solution.py:16
  761.0 74.8 %reduce-scatter.2.cloned.1.call-start = ((), (), s32[]{:S(2)}) async-start(), calls=%async_computation.4 | async-start | bytes 1310720 | tf_op jit(solution)/shard_map/reduce_scatter | solution.py:117
Sparse Core Ops, SparseCore 0:
  8.9 643.6 all-gather.2
  761.1 43.2 all-gather.4
  811.1 24.6 reduce-scatter.1
where the time goes:
time: 843 us; the launch traced here: 842 us
  waiting for transfers between devices  775 us (92%)
  matrix products  24.3 us (3%)
  starting transfers between devices  13.8 us (2%)
  between operations  13.3 us (2%)
    all_gather x1, waiting for transfers between devices, shards(): lax.all_gather(w_query, 'ctx', axis=0, tiled=True)  624 us
    ppermute x28, waiting for transfers between devices, from_behind(): return lax.ppermute(block, axis, route)  69 us
    all_gather x1, waiting for transfers between devices, shards(): gathered = lax.all_gather(normalized, 'ctx', axis=0, tiled=True)  43.4 us
    reduce_scatter x1, waiting for transfers between devices, shards(): lax.psum_scatter(jnp.dot(gathered, w_output, preferred_element_type=jnp.f...  24.8 us
  transfers between devices with their start and end apart: 32, of which 18 were waited for; matrix products, arithmetic and copies ran while one was open for 0% of the time, Pallas kernels for 0%

commit v1 on v0

v1 whole, which is shorter than its diff:
```python
import math

import jax
import jax.numpy as jnp
from jax import lax
from jax.sharding import PartitionSpec as P

H = 64
KVH = 8
HD = 128


def shards(
    hidden, norm_gain, w_query, manifest_keys, manifest_values, w_output, valid_len, home_block
):
    ctx_count = lax.axis_size("ctx")
    ctx_index = lax.axis_index("ctx")
    head_index = lax.axis_index("head")
    rows, feat = hidden.shape
    d_model = feat * ctx_count
    width = w_query.shape[1]
    heads_here = width // HD
    group = H // KVH
    span = manifest_keys.shape[1]
    hsplit = min(ctx_count, heads_here)
    rsplit = ctx_count // hsplit
    rows_dev = rows // rsplit
    heads_dev = heads_here // hsplit

    widened = hidden.astype(jnp.float32)
    total_sq = lax.psum(jnp.sum(widened * widened, axis=1, keepdims=True), "ctx")
    inv_rms = lax.rsqrt(total_sq / d_model + 1e-05)
    gain = lax.dynamic_slice_in_dim(norm_gain, ctx_index * feat, feat, 0)
    normed = (widened * inv_rms * gain[None, :]).astype(jnp.bfloat16)
    partial = jnp.dot(normed, w_query, preferred_element_type=jnp.float32)
    partial = partial.reshape(rsplit, rows_dev, hsplit, heads_dev * HD).transpose(2, 0, 1, 3)
    partial = partial.reshape(ctx_count, rows_dev, heads_dev * HD)
    query = lax.psum_scatter(partial, "ctx", scatter_dimension=0, tiled=False).astype(jnp.bfloat16)

    dest_heads = head_index * heads_here + (jnp.arange(ctx_count) // rsplit) * heads_dev
    dest_kv = dest_heads // group
    kv = jnp.stack([manifest_keys[dest_kv], manifest_values[dest_kv]], axis=1)
    kv = lax.all_to_all(kv, "ctx", split_axis=0, concat_axis=0, tiled=True)
    kv = kv.transpose(1, 0, 2, 3).reshape(2, ctx_count * span, HD)
    keys, values = kv[0], kv[1]

    first_row = (ctx_index % rsplit) * rows_dev
    lens = lax.dynamic_slice_in_dim(valid_len, first_row, rows_dev, 0)
    blocks = lax.dynamic_slice_in_dim(home_block, first_row, rows_dev, 0)
    places = jnp.arange(ctx_count * span, dtype=jnp.int32)
    usable = (places[None, :] < lens[:, None]) | ((places // span)[None, :] == blocks[:, None])
    usable = usable[:, None, :]
    q3 = query.reshape(rows_dev, heads_dev, HD)
    scores = jnp.einsum("nhd,jd->nhj", q3, keys, preferred_element_type=jnp.float32) * (
        1.0 / math.sqrt(HD)
    )
    scores = jnp.where(usable, scores, -1e30)
    row_max = jnp.max(scores, axis=2, keepdims=True)
    expo = jnp.where(usable, jnp.exp(scores - row_max), 0.0)
    row_sum = jnp.sum(expo, axis=2, keepdims=True)
    weighted = jnp.einsum(
        "nhj,jd->nhd", expo.astype(jnp.bfloat16), values, preferred_element_type=jnp.float32
    )
    attn = (weighted / row_sum).astype(jnp.bfloat16).reshape(rows_dev, heads_dev * HD)
    attn = lax.all_gather(attn, "ctx", axis=0, tiled=False)
    attn = attn.reshape(hsplit, rsplit, rows_dev, heads_dev * HD).transpose(1, 2, 0, 3)
    attn = attn.reshape(rows, width)
    return lax.psum_scatter(
        jnp.dot(attn, w_output, preferred_element_type=jnp.float32),
        "head",
        scatter_dimension=0,
        tiled=True,
    )


def solution(mesh):
    in_specs = (
        P(None, "ctx"),
        P(),
        P("ctx", "head"),
        P(None, "ctx", None),
        P(None, "ctx", None),
        P("head", "ctx"),
        P(),
        P(),
    )
    out_specs = P("head", "ctx")
    return jax.shard_map(shards, mesh=mesh, in_specs=in_specs, out_specs=out_specs, check_vma=False)
```

time: 843 us -> 223 us (0.26)
  waiting for transfers between devices: 775 us -> 152 us
  blocking collectives: 0 us -> 18.7 us
  starting transfers between devices: 13.8 us -> 3.69 us
    all_gather x2 -> x1, waiting for transfers between devices: 668 us -> 40.2 us  [shards(): attn = lax.all_gather(attn, 'ctx', axis=0, tiled=False)]
    ppermute x28 -> x0, waiting for transfers between devices: 69 us -> none  [from_behind(): return lax.ppermute(block, axis, route)]
    all_to_all x1, waiting for transfers between devices: 12.7 us -> 61.5 us  [shards(): kv = lax.all_to_all(kv, 'ctx', split_axis=0, concat_axis=0, tiled=True)]
    reduce_scatter x1 -> x2, waiting for transfers between devices: 24.8 us -> 50 us  [the longest x1 25.2 us: shards(): lax.psum_scatter(partial, 'ctx', scatter_dimension=0, tiled=False)]
    psum x0 -> x1, blocking collectives: none -> 18.7 us  [shards(): lax.psum(jnp.sum(widened * widened, axis=1, keepdims=True), 'ctx')]
    dot_general x18 -> x2, matrix products: 24.3 us -> 8.15 us  [the longest x1 4.46 us: shards(): jnp.dot(attn, w_output, preferred_element_type=jnp.float32)]
  transfers between devices with their start and end apart: 32 -> 4, of which waited for: 18 -> 4; matrix products, arithmetic and copies ran while one was open for 0% -> 3% of each run, Pallas kernels for 0% -> 0%
where the time goes in v1:
time: 223 us; the launch traced here: 222 us
  waiting for transfers between devices  152 us (68%)
  matrix products  22 us (10%)
  blocking collectives  18.7 us (8%)
  between operations  13.2 us (6%)
  local copies, waits for them, and re-layouts  7.19 us (3%)
  other arithmetic  5.66 us (3%)
  starting transfers between devices  3.69 us (2%)
    all_to_all x1, waiting for transfers between devices, shards(): kv = lax.all_to_all(kv, 'ctx', split_axis=0, concat_axis=0, tiled=True)  61.5 us
    all_gather x1, waiting for transfers between devices, shards(): attn = lax.all_gather(attn, 'ctx', axis=0, tiled=False)  40.2 us
    reduce_scatter x1, waiting for transfers between devices, shards(): lax.psum_scatter(partial, 'ctx', scatter_dimension=0, tiled=False)  25.2 us
    reduce_scatter x1, waiting for transfers between devices, shards(): lax.psum_scatter(jnp.dot(attn, w_output, preferred_element_type=jnp.float...  24.8 us
    psum x1, blocking collectives, shards(): lax.psum(jnp.sum(widened * widened, axis=1, keepdims=True), 'ctx')  18.7 us
    sub x1, matrix products, shards(): expo = jnp.where(usable, jnp.exp(scores - row_max), 0.0)  8.3 us
    reshape x1, matrix products, shards(): partial.reshape(rsplit, rows_dev, hsplit, heads_dev * HD)  5.51 us
  transfers between devices with their start and end apart: 4, of which 4 were waited for; matrix products, arithmetic and copies ran while one was open for 3% of the time, Pallas kernels for 0%

profile of v1, /device:TPU:1, one launch (start us, length us, event | category | flops | bytes accessed | tf_op | source)
XLA Modules:
  0.0 222.1 jit_solution(15778530597544170264)
XLA Ops:
  6.5 0.0 copy-start
  6.5 0.0 reduce-scatter.3.cloned.1.call-start
  6.5 1.3 fusion.14
  7.9 18.7 %psum.7 = f32[256,1]{0,1:T(1,128)S(1)} all-reduce(f32[256,1]{0,1:T(1,128)S(1)} %bitcast.42), channel_id=1, replica_groups=mesh['ctx'=8,'head'=4] {'ctx'}, use_global_device_ids=true, to_apply=%region_1.0 | all-reduce | flops 256 | bytes 2048 | tf_op jit(solution)/shard_map/psum | solution.py:31
  26.6 0.7 dynamic_slice.2
  27.3 5.5 %fusion.19 = f32[256,2048]{0,1:T(8,128)} fusion(bf16[1024,2048]{1,0:T(8,128)(2,1)} %param.10, bf16[256,1024]{1,0:T(8,128)(2,1)} %param.8, f32[1024]{0:T(1024)S(1)} %dynamic_slice.2, f32[256]{0:T(256)S(1)} %bitcast.43), kind=kOutput, calls=%fused_computation.22 | convolution fusion | flops 1074790400 | bytes 6820864 | tf_op jit(solution)/shard_map/reshape | solution.py:36
  32.8 0.0 reduce-scatter.3.cloned.1.call-update
  32.8 0.0 copy-done
  32.9 0.7 gather_fusion.1
  33.6 2.0 gather_fusion
  35.6 0.0 copy-start.2
  35.6 0.0 copy-start.3
  35.6 1.5 pad_maximum_fusion
  37.1 3.6 %all-to-all-start = ((bf16[8,2,512,128]{3,2,1,0:T(8,128)(2,1)}), bf16[8,2,512,128]{3,2,1,0:T(8,128)(2,1)S(1)}, u32[]{:S(2)}, u32[]{:S(2)}) async-start(bf16[8,2,512,128]{3,2,1,0:T(8,128)(2,1)} %pad_maximum_fusion), calls=%async_computation.1 | async-start | bytes 4194304 | tf_op jit(solution)/shard_map/all_to_all | solution.py:43
  40.7 0.0 all-gather.2.cloned.1.call-start
  40.8 0.0 copy-done.2
  40.8 0.0 copy-done.3
  40.8 1.9 fusion.6
  42.7 61.5 %all-to-all-done = bf16[8,2,512,128]{3,2,1,0:T(8,128)(2,1)S(1)} async-done(((bf16[8,2,512,128]{3,2,1,0:T(8,128)(2,1)}), bf16[8,2,512,128]{3,2,1,0:T(8,128)(2,1)S(1)}, u32[]{:S(2)}, u32[]{:S(2)}) %all-to-all-start) | async-done | bytes 2097184 | tf_op jit(solution)/shard_map/all_to_all | solution.py:43
  104.1 1.5 fusion.29
  105.6 25.2 %reduce-scatter.3.cloned.1.call-done = f32[1,256,256]{1,2,0:T(8,128)} async-done(((f32[8,256,256]{1,2,0:T(8,128)}), f32[1,256,256]{1,2,0:T(8,128)}) %reduce-scatter.3.cloned.1.call-update) | async-done | bytes 262160 | tf_op jit(solution)/shard_map/reduce_scatter | solution.py:38
  130.8 1.0 convert_element_type.21
  131.8 0.0 copy-start.1
  131.8 8.3 %fusion.30 = (f32[256,2]{0,1:T(2,128)S(1)}, bf16[256,2,4096]{2,0,1:T(8,128)(2,1)}) fusion(pred[256,4096]{1,0:T(8,128)(4,1)} %fusion.6, bf16[256,2,128]{0,2,1:T(8,128)(2,1)S(1)} %bitcast.41, bf16[4096,128,1]{1,0,2:T(8,128)(2,1)} %bitcast.39), kind=kOutput, calls=%fused_computation.43 | convolution fusion | flops 549457920 | bytes 6424576 | tf_op jit(solution)/shard_map/sub | solution.py:59
  140.1 0.0 copy-done.1
  140.1 3.7 %fusion.11 = bf16[256,2,128]{0,2,1:T(8,128)(2,1)S(1)} fusion(bf16[4096,128,1]{1,0,2:T(8,128)(2,1)S(1)} %bitcast.34, bf16[256,2,4096]{2,0,1:T(8,128)(2,1)} %get-tuple-element.8, f32[256,2]{0,1:T(2,128)S(1)} %get-tuple-element.7), kind=kOutput, calls=%fused_computation.17 | convolution fusion | flops 537001984 | bytes 5376000 | tf_op jit(solution)/shard_map/nhj,jd->nhd/dot_general | solution.py:61
  143.8 0.8 copy.20
  144.6 0.0 all-gather.2.cloned.1.call-update
  144.6 0.0 reduce-scatter.5.cloned.1.call-start
  144.6 40.2 %all-gather.2.cloned.1.call-done = bf16[8,256,256]{2,1,0:T(8,128)(2,1)} async-done(((bf16[1,256,256]{2,1,0:T(8,128)(2,1)}), bf16[8,256,256]{2,1,0:T(8,128)(2,1)}) %all-gather.2.cloned.1.call-update) | async-done | bytes 1048592 | tf_op jit(solution)/shard_map/all_gather | solution.py:65
  184.8 1.5 copy.21
  186.3 4.5 %fusion.31 = f32[256,1024]{1,0:T(8,128)} fusion(bf16[256,2048]{0,1:T(8,128)(2,1)S(1)} %bitcast.38, bf16[2048,1024]{1,0:T(8,128)(2,1)} %param.13), kind=kOutput, calls=%fused_computation.44 | convolution fusion | flops 1073741824 | bytes 6291456 | tf_op jit(solution)/shard_map/dot_general | solution.py:69
  190.7 0.0 reduce-scatter.5.cloned.1.call-update
  190.8 24.8 %reduce-scatter.5.cloned.1.call-done = f32[64,1024]{1,0:T(8,128)} async-done(((f32[256,1024]{1,0:T(8,128)}), f32[64,1024]{1,0:T(8,128)}) %reduce-scatter.5.cloned.1.call-update) | async-done | bytes 262160 | tf_op jit(solution)/shard_map/reduce_scatter | solution.py:68
  (4 shorter events, 0.0 us)
Async XLA Ops:
  6.5 26.3 %copy-start = (bf16[8,512,128]{2,1,0:T(8,128)(2,1)S(1)}, bf16[8,512,128]{2,1,0:T(8,128)(2,1)}, u32[]{:S(2)}) copy-start(bf16[8,512,128]{2,1,0:T(8,128)(2,1)} %param.12) | copy-start | bytes 3145732
  6.5 124.3 %reduce-scatter.3.cloned.1.call-start = ((), (), s32[]{:S(2)}) async-start(), calls=%async_computation.3 | async-start | bytes 2359296 | tf_op jit(solution)/shard_map/reduce_scatter | solution.py:38
  35.6 5.2 %copy-start.2 = (s32[256]{0:T(256)S(1)}, s32[256]{0:T(256)}, u32[]{:S(2)}) copy-start(s32[256]{0:T(256)} %param.14) | copy-start | bytes 3076
  35.6 5.2 %copy-start.3 = (s32[256]{0:T(256)S(1)}, s32[256]{0:T(256)}, u32[]{:S(2)}) copy-start(s32[256]{0:T(256)} %param.15) | copy-start | bytes 3076
  37.1 67.0 %all-to-all-start = ((bf16[8,2,512,128]{3,2,1,0:T(8,128)(2,1)}), bf16[8,2,512,128]{3,2,1,0:T(8,128)(2,1)S(1)}, u32[]{:S(2)}, u32[]{:S(2)}) async-start(bf16[8,2,512,128]{3,2,1,0:T(8,128)(2,1)} %pad_maximum_fusion), calls=%async_computation.1 | async-start | bytes 4194304 | tf_op jit(solution)/shard_map/all_to_all | solution.py:43
  40.7 144.1 %all-gather.2.cloned.1.call-start = ((), (), s32[]{:S(2)}) async-start(), calls=%async_computation.4 | async-start | bytes 1179648 | tf_op jit(solution)/shard_map/all_gather | solution.py:65
  131.8 8.3 %copy-start.1 = (bf16[1,8,512,128]{3,2,0,1:T(8,128)(2,1)S(1)}, bf16[1,8,512,128]{3,2,0,1:T(8,128)(2,1)}, u32[]{:S(2)}) copy-start(bf16[1,8,512,128]{3,2,0,1:T(8,128)(2,1)} %get-tuple-element.6) | copy-start | bytes 3145732
  144.6 71.0 %reduce-scatter.5.cloned.1.call-start = ((), (), s32[]{:S(2)}) async-start(), calls=%async_computation.5 | async-start | bytes 1310720 | tf_op jit(solution)/shard_map/reduce_scatter | solution.py:68
Sparse Core Ops, SparseCore 0:
  32.9 97.8 reduce-scatter.2
  144.7 40.0 all-gather.1
  190.9 24.6 reduce-scatter.4

commit v2 on v1

--- a/solution.py
+++ b/solution.py
@@ -3,11 +3,253 @@
 import jax
 import jax.numpy as jnp
 from jax import lax
+from jax.experimental import pallas as pl
+from jax.experimental.pallas import tpu as pltpu
 from jax.sharding import PartitionSpec as P
 
 H = 64
 KVH = 8
 HD = 128
+
+Z = 4
+X = 2
+
+
+def fused_kernel(
+    hidden, gain, wq_hbm, k_hbm, v_hbm, wo_hbm, lens, home, out,
+    wq, wo, kb, vb, vt, nrm, sq, xsend, xrecv, qown, zsend, zrecv, qb, sc,
+    os_, st, ocr, scr, az, ax, acc, orecv, local_sem, send_sem, recv_sem,
+):
+    c = lax.axis_index("ctx")
+    h = lax.axis_index("head")
+    z, x = lax.div(c, X), lax.rem(c, X)
+    nz = lax.axis_size("ctx")
+    nh = lax.axis_size("head")
+    rows, feat = hidden.shape
+    span = kb.shape[1]
+    chunk = qb.shape[2]
+    half = chunk * Z
+    out_rows = out.shape[0]
+    per_chunk = chunk // HD
+    scale = 1.0 / math.sqrt(HD)
+    f32 = jnp.float32
+    pending = []
+    next_sem = [0]
+
+    def at(zz, xx):
+        return zz * X + xx
+
+    def send(src, dst, **where):
+        i = next_sem[0]
+        next_sem[0] += 1
+        copy = pltpu.make_async_remote_copy(
+            src_ref=src, dst_ref=dst, send_sem=send_sem.at[i], recv_sem=recv_sem.at[i],
+            device_id=where, device_id_type=pl.DeviceIdType.MESH,
+        )
+        copy.start()
+        pending.append(copy)
+        return copy
+
+    def zat(k):
+        return lax.rem(z + k, Z)
+
+    barrier = pltpu.get_barrier_semaphore()
+    for k in range(1, nz):
+        pl.semaphore_signal(barrier, inc=1, device_id={"ctx": lax.rem(c + k, nz)}, device_id_type=pl.DeviceIdType.MESH)
+    for k in range(1, nh):
+        pl.semaphore_signal(barrier, inc=1, device_id={"head": lax.rem(h + k, nh)}, device_id_type=pl.DeviceIdType.MESH)
+
+    kv_mine = h * X + x
+    kv_other = h * X + (1 - x)
+    locals_ = [
+        pltpu.make_async_copy(wq_hbm, wq, local_sem.at[0]),
+        pltpu.make_async_copy(k_hbm.at[kv_mine], kb.at[0], local_sem.at[1]),
+        pltpu.make_async_copy(v_hbm.at[kv_mine], vb.at[0], local_sem.at[2]),
+        pltpu.make_async_copy(wo_hbm, wo, local_sem.at[3]),
+    ]
+    for cp in locals_:
+        cp.start()
+
+    eye = lax.broadcasted_iota(jnp.int32, (128, 128), 0) == lax.broadcasted_iota(jnp.int32, (128, 128), 1)
+    wide = hidden[...].astype(f32)
+    col = jnp.sum(wide * wide, axis=1, keepdims=True)
+    pieces = [
+        jnp.sum(jnp.where(eye, col[b * 128 : (b + 1) * 128], 0.0), axis=0, keepdims=True)
+        for b in range(rows // 128)
+    ]
+    pieces.append(jnp.zeros((8 - rows // 128, 128), f32))
+    sq[0] = jnp.concatenate(pieces, axis=0)
+    pl.semaphore_wait(barrier, nz - 1 + nh - 1)
+    sq_copies = [send(sq.at[0], sq.at[k], ctx=lax.rem(c + k, nz)) for k in range(1, nz)]
+    zp = z + 1 - 2 * lax.rem(z, 2)
+    kv_copies = []
+    for slot, (idx, zz, xx) in enumerate(((kv_other, z, 1 - x), (kv_mine, zp, x), (kv_other, zp, 1 - x)), 1):
+        kv_copies.append(send(k_hbm.at[idx], kb.at[slot], ctx=at(zz, xx)))
+        kv_copies.append(send(v_hbm.at[idx], vb.at[slot], ctx=at(zz, xx)))
+    for cp in sq_copies:
+        cp.wait_recv()
+    total = sq[0]
+    for k in range(1, nz):
+        total = total + sq[k]
+    inv = lax.rsqrt(total / (feat * nz) + 1e-05)
+    for b in range(rows // 128):
+        inv_col = jnp.sum(jnp.where(eye, inv[b : b + 1, :], 0.0), axis=1, keepdims=True)
+        blk = hidden[b * 128 : (b + 1) * 128, :].astype(f32)
+        g = gain[:, pl.ds(pl.multiple_of(c * feat, feat), feat)]
+        nrm[b * 128 : (b + 1) * 128, :] = (blk * inv_col * g).astype(jnp.bfloat16)
+
+    def part(xx, k):
+        cols = pl.ds(pl.multiple_of(xx * half + zat(k) * chunk, chunk), chunk)
+        return jnp.dot(nrm[...], wq[:, cols], preferred_element_type=f32)
+
+    locals_[0].wait()
+    x_copies = {}
+    for k in (1, 2, 3, 0):
+        xsend[k] = part(1 - x, k)
+        x_copies[k] = send(xsend.at[k], xrecv.at[k], ctx=at(z, 1 - x))
+    for k in (1, 2, 3, 0):
+        qown[k] = part(x, k)
+    z_copies = []
+    for k in (1, 2, 3):
+        x_copies[k].wait_recv()
+        zsend[k - 1] = qown[k] + xrecv[k]
+        z_copies.append(send(zsend.at[k - 1], zrecv.at[k - 1], ctx=at(zat(k), x)))
+
+    locals_[1].wait()
+    locals_[2].wait()
+    for cp in kv_copies:
+        cp.wait_recv()
+    for s in range(4):
+        vt[s] = vb[s].astype(f32).T.astype(jnp.bfloat16)
+
+    x_copies[0].wait_recv()
+    qsum = qown[0] + xrecv[0]
+    for k in range(3):
+        z_copies[k].wait_recv()
+        qsum = qsum + zrecv[k]
+    qb[0] = qsum.astype(jnp.bfloat16)
+    far = at(zat(2), x)
+    q_copy = send(qb.at[0], qb.at[1], ctx=far)
+
+    place = lax.broadcasted_iota(jnp.int32, (span, rows), 0)
+    owners = (at(z, x), at(z, 1 - x), at(zp, x), at(zp, 1 - x))
+
+    def attend(i):
+        for j in range(per_chunk):
+            q_head = qb[i, :, j * HD : (j + 1) * HD]
+            top = jnp.full((1, rows), -1e30, f32)
+            for s in range(4):
+                limit = jnp.where(home[...] == owners[s], span, lens[...] - owners[s] * span)
+                raw = lax.dot_general(kb[s], q_head, (((1,), (1,)), ((), ())), preferred_element_type=f32)
+                raw = jnp.where(place < limit, raw, -1e30)
+                sc[s] = raw
+                top = jnp.maximum(top, jnp.max(raw, axis=0, keepdims=True))
+            tot = jnp.zeros((1, rows), f32)
+            acc_o = jnp.zeros((HD, rows), f32)
+            for s in range(4):
+                e = jnp.exp((sc[s] - top) * scale)
+                tot = tot + jnp.sum(e, axis=0, keepdims=True)
+                acc_o = acc_o + jnp.dot(vt[s], e.astype(jnp.bfloat16), preferred_element_type=f32)
+            os_[i, j] = acc_o
+            st[i, j : j + 1, :] = top
+            st[i, per_chunk + j : per_chunk + j + 1, :] = tot
+
+    st[...] = jnp.zeros_like(st)
+    attend(0)
+    q_copy.wait_recv()
+    attend(1)
+    o_copy = send(os_.at[1], ocr, ctx=far)
+    s_copy = send(st.at[1], scr, ctx=far)
+    o_copy.wait_recv()
+    s_copy.wait_recv()
+    for j in range(per_chunk):
+        m0, m1 = st[0, j : j + 1, :], scr[j : j + 1, :]
+        l0, l1 = st[0, per_chunk + j : per_chunk + j + 1, :], scr[per_chunk + j : per_chunk + j + 1, :]
+        m = jnp.maximum(m0, m1)
+        a0, a1 = jnp.exp((m0 - m) * scale), jnp.exp((m1 - m) * scale)
+        res = (a0 * os_[0, j] + a1 * ocr[j]) / (a0 * l0 + a1 * l1)
+        az[0, :, j * HD : (j + 1) * HD] = res.T.astype(jnp.bfloat16)
+
+    ax_copies = [send(az.at[0], ax.at[0], ctx=at(z, 1 - x))]
+    az_copies = [send(az.at[0], az.at[k], ctx=at(zat(k), x)) for k in range(1, Z)]
+
+    def project(piece, xx, k):
+        first = pl.multiple_of(xx * half + zat(Z - k) * chunk, chunk)
+        return jnp.dot(piece, wo[pl.ds(first, chunk), :], preferred_element_type=f32)
+
+    locals_[3].wait()
+    acc[...] = project(az[0], x, 0)
+    for k in range(1, Z):
+        az_copies[k - 1].wait_recv()
+        ax_copies.append(send(az.at[k], ax.at[k], ctx=at(z, 1 - x)))
+        acc[...] += project(az[k], x, k)
+    for k in range(Z):
+        ax_copies[k].wait_recv()
+        acc[...] += project(ax[k], 1 - x, k)
+    out_copies = []
+    for d in range(1, nh):
+        dest = lax.rem(h + d, nh)
+        piece = acc.at[pl.ds(pl.multiple_of(dest * out_rows, out_rows), out_rows), :]
+        out_copies.append(send(piece, orecv.at[d - 1], head=dest))
+    mine = acc[pl.ds(pl.multiple_of(h * out_rows, out_rows), out_rows), :]
+    for d in range(nh - 1):
+        out_copies[d].wait_recv()
+        mine = mine + orecv[d]
+    out[...] = mine
+    for cp in pending:
+        cp.wait_send()
+
+
+def fused(hidden, norm_gain, w_query, keys, values, w_output, valid_len, home_block):
+    rows, feat = hidden.shape
+    width = w_query.shape[1]
+    cols = w_output.shape[1]
+    nz, nh = lax.axis_size("ctx"), lax.axis_size("head")
+    span = keys.shape[1]
+    chunk = width // nz
+    bf16, f32 = jnp.bfloat16, jnp.float32
+    n_copies = (nz - 1) + 6 + 4 + 3 + 1 + 2 + 1 + 3 + 3 + (nh - 1)
+    vmem = pl.BlockSpec(memory_space=pltpu.VMEM)
+    hbm = pl.BlockSpec(memory_space=pl.ANY)
+    return pl.pallas_call(
+        fused_kernel,
+        out_shape=jax.ShapeDtypeStruct((rows // nh, cols), f32),
+        in_specs=[vmem, vmem, hbm, hbm, hbm, hbm, vmem, vmem],
+        out_specs=vmem,
+        scratch_shapes=[
+            pltpu.VMEM(w_query.shape, bf16),
+            pltpu.VMEM(w_output.shape, bf16),
+            pltpu.VMEM((4, span, HD), bf16),
+            pltpu.VMEM((4, span, HD), bf16),
+            pltpu.VMEM((4, HD, span), bf16),
+            pltpu.VMEM((rows, feat), bf16),
+            pltpu.VMEM((nz, 8, 128), f32),
+            pltpu.VMEM((Z, rows, chunk), f32),
+            pltpu.VMEM((Z, rows, chunk), f32),
+            pltpu.VMEM((Z, rows, chunk), f32),
+            pltpu.VMEM((Z - 1, rows, chunk), f32),
+            pltpu.VMEM((Z - 1, rows, chunk), f32),
+            pltpu.VMEM((2, rows, chunk), bf16),
+            pltpu.VMEM((4, span, rows), f32),
+            pltpu.VMEM((2, chunk // HD, HD, rows), f32),
+            pltpu.VMEM((2, 8, rows), f32),
+            pltpu.VMEM((chunk // HD, HD, rows), f32),
+            pltpu.VMEM((8, rows), f32),
+            pltpu.VMEM((Z, rows, chunk), bf16),
+            pltpu.VMEM((Z, rows, chunk), bf16),
+            pltpu.VMEM((rows, cols), f32),
+            pltpu.VMEM((nh - 1, rows // nh, cols), f32),
+            pltpu.SemaphoreType.DMA((4,)),
+            pltpu.SemaphoreType.DMA((n_copies,)),
+            pltpu.SemaphoreType.DMA((n_copies,)),
+        ],
+        compiler_params=pltpu.CompilerParams(
+            collective_id=0, has_side_effects=True, vmem_limit_bytes=48 * 1024 * 1024
+        ),
+    )(
+        hidden, norm_gain.reshape(1, -1), w_query, keys, values, w_output,
+        valid_len.reshape(1, -1), home_block.reshape(1, -1),
+    )
 
 
 def shards(
@@ -85,4 +327,5 @@
         P(),
     )
     out_specs = P("head", "ctx")
-    return jax.shard_map(shards, mesh=mesh, in_specs=in_specs, out_specs=out_specs, check_vma=False)
+    small = mesh.shape["ctx"] == Z * X and mesh.shape["head"] * X == KVH
+    return jax.shard_map(fused if small else shards, mesh=mesh, in_specs=in_specs, out_specs=out_specs, check_vma=False)

time: 223 us -> 103 us (0.46)
  waiting for transfers between devices: 152 us -> 0 us
  Pallas kernels: 0 us -> 96.6 us
  matrix products: 22 us -> 0 us
  blocking collectives: 18.7 us -> 0 us
  between operations: 13.2 us -> 0.02 us
  other arithmetic: 5.66 us -> 0 us
  starting transfers between devices: 3.69 us -> 0 us
    pallas_call x0 -> x1, Pallas kernels: none -> 96.6 us  [fused(): pl.pallas_call(fused_kernel, out_shape=jax.ShapeDtypeStruct((rows // nh,...]
    all_to_all x1 -> x0, waiting for transfers between devices: 61.5 us -> none  [shards(): kv = lax.all_to_all(kv, 'ctx', split_axis=0, concat_axis=0, tiled=True)]
    reduce_scatter x2 -> x0, waiting for transfers between devices: 50 us -> none  [the longest x1 25.2 us: shards(): lax.psum_scatter(partial, 'ctx', scatter_dimension=0, tiled=False)]
    all_gather x1 -> x0, waiting for transfers between devices: 40.2 us -> none  [shards(): attn = lax.all_gather(attn, 'ctx', axis=0, tiled=False)]
    psum x1 -> x0, blocking collectives: 18.7 us -> none  [shards(): lax.psum(jnp.sum(widened * widened, axis=1, keepdims=True), 'ctx')]
    sub x1 -> x0, matrix products: 8.3 us -> none  [shards(): expo = jnp.where(usable, jnp.exp(scores - row_max), 0.0)]
    dot_general x2 -> x0, matrix products: 8.15 us -> none  [the longest x1 4.46 us: shards(): jnp.dot(attn, w_output, preferred_element_type=jnp.float32)]
    unnamed x8 -> x13, local copies, waits for them, and re-layouts: 0.02 us -> 6.31 us
  transfers between devices with their start and end apart: 4 -> 0, of which waited for: 4 -> 0; matrix products, arithmetic and copies ran while one was open for 3% -> 0% of each run, Pallas kernels for 0% -> 0%
where the time goes in v2:
time: 103 us
  Pallas kernels  96.6 us (94%)
  local copies, waits for them, and re-layouts  6.31 us (6%)
    pallas_call x1, Pallas kernels, fused(): pl.pallas_call(fused_kernel, out_shape=jax.ShapeDtypeStruct((rows // nh,...  96.6 us
    unnamed x13, local copies, waits for them, and re-layouts  6.31 us

profile of v2, /device:TPU:1, one launch (start us, length us, event | category | flops | bytes accessed | tf_op | source)
XLA Modules:
  0.0 102.9 jit_solution(3449737566027874564)
XLA Ops:
  0.0 0.0 copy-start
  0.0 1.2 %copy-done = bf16[8,512,128]{2,1,0:T(8,128)(2,1)S(1)} copy-done((bf16[8,512,128]{2,1,0:T(8,128)(2,1)S(1)}, bf16[8,512,128]{2,1,0:T(8,128)(2,1)}, u32[]{:S(2)}) %copy-start) | copy-done | bytes 1048600
  1.2 0.0 copy-start.1
  1.2 1.2 %copy-done.1 = bf16[8,512,128]{2,1,0:T(8,128)(2,1)S(1)} copy-done((bf16[8,512,128]{2,1,0:T(8,128)(2,1)S(1)}, bf16[8,512,128]{2,1,0:T(8,128)(2,1)}, u32[]{:S(2)}) %copy-start.1) | copy-done | bytes 1048600
  2.5 0.0 copy-start.2
  2.5 1.0 %copy-done.2 = bf16[256,1024]{1,0:T(8,128)(2,1)S(1)} copy-done((bf16[256,1024]{1,0:T(8,128)(2,1)S(1)}, bf16[256,1024]{1,0:T(8,128)(2,1)}, u32[]{:S(2)}) %copy-start.2) | copy-done | bytes 524312
  3.5 0.0 copy-start.3
  3.5 0.8 copy-done.3
  4.3 0.0 copy-start.4
  4.3 0.7 copy-done.4
  4.9 0.0 copy-start.5
  4.9 0.7 copy-done.5
  5.6 96.6 %shard_map.82 = f32[64,1024]{1,0:T(8,128)S(1)} custom-call(bf16[256,1024]{1,0:T(8,128)(2,1)S(1)} %copy-done.2, f32[1,8192]{1,0:T(1,128)S(1)} %bitcast.3, bf16[1024,2048]{1,0:T(8,128)(2,1)} %wq_hbm.1, bf16[8,512,128]{2,1,0:T(8,128)(2,1)S(1)} %copy-done, bf16[8,512,128]{2,1,0:T(8,128)(2,1)S(1)} %copy-done.1, bf16[2048,1024]{1,0:T(8,128)(2,1)} %wo_hbm.1, ...), custom_call_target="tpu_custom_call" | custom-call | tf_op jit(solution)/shard_map/pallas_call | solution.py:214
  102.2 0.7 copy.10
Async XLA Ops:
  0.0 1.2 %copy-start = (bf16[8,512,128]{2,1,0:T(8,128)(2,1)S(1)}, bf16[8,512,128]{2,1,0:T(8,128)(2,1)}, u32[]{:S(2)}) copy-start(bf16[8,512,128]{2,1,0:T(8,128)(2,1)} %k_hbm.1) | copy-start | bytes 3145732
  1.2 1.2 %copy-start.1 = (bf16[8,512,128]{2,1,0:T(8,128)(2,1)S(1)}, bf16[8,512,128]{2,1,0:T(8,128)(2,1)}, u32[]{:S(2)}) copy-start(bf16[8,512,128]{2,1,0:T(8,128)(2,1)} %v_hbm.1) | copy-start | bytes 3145732
  2.5 1.0 %copy-start.2 = (bf16[256,1024]{1,0:T(8,128)(2,1)S(1)}, bf16[256,1024]{1,0:T(8,128)(2,1)}, u32[]{:S(2)}) copy-start(bf16[256,1024]{1,0:T(8,128)(2,1)} %hidden.1) | copy-start | bytes 1572868
  3.5 0.8 copy-start.3
  4.3 0.7 copy-start.4
  4.9 0.7 copy-start.5

commit v3 on v2

--- a/solution.py
+++ b/solution.py
@@ -18,7 +18,7 @@
 def fused_kernel(
     hidden, gain, wq_hbm, k_hbm, v_hbm, wo_hbm, lens, home, out,
     wq, wo, kb, vb, vt, nrm, sq, xsend, xrecv, qown, zsend, zrecv, qb, sc,
-    os_, st, ocr, scr, az, ax, acc, orecv, local_sem, send_sem, recv_sem,
+    os_, st, ocr, scr, az, ax, acc, orecv, ysend, local_sem, send_sem, recv_sem,
 ):
     c = lax.axis_index("ctx")
     h = lax.axis_index("head")
@@ -28,7 +28,6 @@
     rows, feat = hidden.shape
     span = kb.shape[1]
     chunk = qb.shape[2]
-    half = chunk * Z
     out_rows = out.shape[0]
     per_chunk = chunk // HD
     scale = 1.0 / math.sqrt(HD)
@@ -59,8 +58,7 @@
     for k in range(1, nh):
         pl.semaphore_signal(barrier, inc=1, device_id={"head": lax.rem(h + k, nh)}, device_id_type=pl.DeviceIdType.MESH)
 
-    kv_mine = h * X + x
-    kv_other = h * X + (1 - x)
+    kv_mine = h * X + lax.div(z, X)
     locals_ = [
         pltpu.make_async_copy(wq_hbm, wq, local_sem.at[0]),
         pltpu.make_async_copy(k_hbm.at[kv_mine], kb.at[0], local_sem.at[1]),
@@ -81,11 +79,11 @@
     sq[0] = jnp.concatenate(pieces, axis=0)
     pl.semaphore_wait(barrier, nz - 1 + nh - 1)
     sq_copies = [send(sq.at[0], sq.at[k], ctx=lax.rem(c + k, nz)) for k in range(1, nz)]
-    zp = z + 1 - 2 * lax.rem(z, 2)
     kv_copies = []
-    for slot, (idx, zz, xx) in enumerate(((kv_other, z, 1 - x), (kv_mine, zp, x), (kv_other, zp, 1 - x)), 1):
-        kv_copies.append(send(k_hbm.at[idx], kb.at[slot], ctx=at(zz, xx)))
-        kv_copies.append(send(v_hbm.at[idx], vb.at[slot], ctx=at(zz, xx)))
+    for k in range(1, Z):
+        idx = h * X + lax.div(zat(k), X)
+        kv_copies.append(send(k_hbm.at[idx], kb.at[k], ctx=at(zat(k), x)))
+        kv_copies.append(send(v_hbm.at[idx], vb.at[k], ctx=at(zat(k), x)))
     for cp in sq_copies:
         cp.wait_recv()
     total = sq[0]
@@ -99,7 +97,7 @@
         nrm[b * 128 : (b + 1) * 128, :] = (blk * inv_col * g).astype(jnp.bfloat16)
 
     def part(xx, k):
-        cols = pl.ds(pl.multiple_of(xx * half + zat(k) * chunk, chunk), chunk)
+        cols = pl.ds(pl.multiple_of(at(zat(k), xx) * chunk, chunk), chunk)
         return jnp.dot(nrm[...], wq[:, cols], preferred_element_type=f32)
 
     locals_[0].wait()
@@ -119,7 +117,7 @@
     locals_[2].wait()
     for cp in kv_copies:
         cp.wait_recv()
-    for s in range(4):
+    for s in range(Z):
         vt[s] = vb[s].astype(f32).T.astype(jnp.bfloat16)
 
     x_copies[0].wait_recv()
@@ -128,17 +126,18 @@
         z_copies[k].wait_recv()
         qsum = qsum + zrecv[k]
     qb[0] = qsum.astype(jnp.bfloat16)
-    far = at(zat(2), x)
-    q_copy = send(qb.at[0], qb.at[1], ctx=far)
+    beside = at(z, 1 - x)
+    q_copy = send(qb.at[0], qb.at[1], ctx=beside)
 
     place = lax.broadcasted_iota(jnp.int32, (span, rows), 0)
-    owners = (at(z, x), at(z, 1 - x), at(zp, x), at(zp, 1 - x))
+    owners = [at(zat(Z - k), x) for k in range(Z)]
 
     def attend(i):
+        copies = []
         for j in range(per_chunk):
             q_head = qb[i, :, j * HD : (j + 1) * HD]
             top = jnp.full((1, rows), -1e30, f32)
-            for s in range(4):
+            for s in range(Z):
                 limit = jnp.where(home[...] == owners[s], span, lens[...] - owners[s] * span)
                 raw = lax.dot_general(kb[s], q_head, (((1,), (1,)), ((), ())), preferred_element_type=f32)
                 raw = jnp.where(place < limit, raw, -1e30)
@@ -146,56 +145,72 @@
                 top = jnp.maximum(top, jnp.max(raw, axis=0, keepdims=True))
             tot = jnp.zeros((1, rows), f32)
             acc_o = jnp.zeros((HD, rows), f32)
-            for s in range(4):
+            for s in range(Z):
                 e = jnp.exp((sc[s] - top) * scale)
                 tot = tot + jnp.sum(e, axis=0, keepdims=True)
                 acc_o = acc_o + jnp.dot(vt[s], e.astype(jnp.bfloat16), preferred_element_type=f32)
             os_[i, j] = acc_o
-            st[i, j : j + 1, :] = top
-            st[i, per_chunk + j : per_chunk + j + 1, :] = tot
+            st[i, j, 0:1, :] = top
+            st[i, j, 1:2, :] = tot
+            if i == 1:
+                copies.append(send(os_.at[1, j], ocr.at[j], ctx=beside))
+                copies.append(send(st.at[1, j], scr.at[j], ctx=beside))
+        return copies
 
     st[...] = jnp.zeros_like(st)
     attend(0)
     q_copy.wait_recv()
-    attend(1)
-    o_copy = send(os_.at[1], ocr, ctx=far)
-    s_copy = send(st.at[1], scr, ctx=far)
-    o_copy.wait_recv()
-    s_copy.wait_recv()
+    state_copies = attend(1)
+    ax_copies, az_copies = {}, {}
     for j in range(per_chunk):
-        m0, m1 = st[0, j : j + 1, :], scr[j : j + 1, :]
-        l0, l1 = st[0, per_chunk + j : per_chunk + j + 1, :], scr[per_chunk + j : per_chunk + j + 1, :]
+        state_copies[2 * j].wait_recv()
+        state_copies[2 * j + 1].wait_recv()
+        m0, m1 = st[0, j, 0:1, :], scr[j, 0:1, :]
+        l0, l1 = st[0, j, 1:2, :], scr[j, 1:2, :]
         m = jnp.maximum(m0, m1)
         a0, a1 = jnp.exp((m0 - m) * scale), jnp.exp((m1 - m) * scale)
         res = (a0 * os_[0, j] + a1 * ocr[j]) / (a0 * l0 + a1 * l1)
-        az[0, :, j * HD : (j + 1) * HD] = res.T.astype(jnp.bfloat16)
-
-    ax_copies = [send(az.at[0], ax.at[0], ctx=at(z, 1 - x))]
-    az_copies = [send(az.at[0], az.at[k], ctx=at(zat(k), x)) for k in range(1, Z)]
-
-    def project(piece, xx, k):
-        first = pl.multiple_of(xx * half + zat(Z - k) * chunk, chunk)
-        return jnp.dot(piece, wo[pl.ds(first, chunk), :], preferred_element_type=f32)
+        az[j, 0] = res.T.astype(jnp.bfloat16)
+        for k in range(1, Z):
+            az_copies[j, k] = send(az.at[j, 0], az.at[j, k], ctx=at(zat(k), x))
+        ax_copies[j, 0] = send(az.at[j, 0], ax.at[j, 0], ctx=beside)
+
+    def project(piece, xx, j, k):
+        first = pl.multiple_of(at(zat(Z - k), xx) * chunk + j * HD, HD)
+        return jnp.dot(piece, wo[pl.ds(first, HD), :], preferred_element_type=f32)
 
     locals_[3].wait()
-    acc[...] = project(az[0], x, 0)
-    for k in range(1, Z):
-        az_copies[k - 1].wait_recv()
-        ax_copies.append(send(az.at[k], ax.at[k], ctx=at(z, 1 - x)))
-        acc[...] += project(az[k], x, k)
-    for k in range(Z):
-        ax_copies[k].wait_recv()
-        acc[...] += project(ax[k], 1 - x, k)
-    out_copies = []
-    for d in range(1, nh):
-        dest = lax.rem(h + d, nh)
-        piece = acc.at[pl.ds(pl.multiple_of(dest * out_rows, out_rows), out_rows), :]
-        out_copies.append(send(piece, orecv.at[d - 1], head=dest))
-    mine = acc[pl.ds(pl.multiple_of(h * out_rows, out_rows), out_rows), :]
-    for d in range(nh - 1):
-        out_copies[d].wait_recv()
-        mine = mine + orecv[d]
-    out[...] = mine
+    for j in range(per_chunk):
+        if j == 0:
+            acc[...] = project(az[j, 0], x, j, 0)
+        else:
+            acc[...] += project(az[j, 0], x, j, 0)
+    for j in range(per_chunk):
+        for k in range(1, Z):
+            az_copies[j, k].wait_recv()
+            ax_copies[j, k] = send(az.at[j, k], ax.at[j, k], ctx=beside)
+            acc[...] += project(az[j, k], x, j, k)
+    for j in range(per_chunk):
+        for k in range(Z):
+            ax_copies[j, k].wait_recv()
+            acc[...] += project(ax[j, k], 1 - x, j, k)
+
+    y, core = lax.div(h, 2), lax.rem(h, 2)
+
+    def rows_of(head):
+        return pl.ds(pl.multiple_of(head * out_rows, out_rows), out_rows)
+
+    other_core = y * 2 + 1 - core
+    other_y = (1 - y) * 2 + core
+    first_core = send(acc.at[rows_of((1 - y) * 2 + 1 - core), :], orecv.at[0], head=other_core)
+    second_core = send(acc.at[rows_of(other_core), :], orecv.at[1], head=other_core)
+    first_core.wait_recv()
+    ysend[...] = acc[rows_of(other_y), :] + orecv[0]
+    y_copy = send(ysend, orecv.at[2], head=other_y)
+    second_core.wait_recv()
+    mine = acc[rows_of(h), :] + orecv[1]
+    y_copy.wait_recv()
+    out[...] = mine + orecv[2]
     for cp in pending:
         cp.wait_send()
 
@@ -208,9 +223,10 @@
     span = keys.shape[1]
     chunk = width // nz
     bf16, f32 = jnp.bfloat16, jnp.float32
-    n_copies = (nz - 1) + 6 + 4 + 3 + 1 + 2 + 1 + 3 + 3 + (nh - 1)
+    per = chunk // HD
+    n_copies = (nz - 1) + 6 + 4 + 3 + 1 + 2 * per + 7 * per + 3
     vmem = pl.BlockSpec(memory_space=pltpu.VMEM)
-    hbm = pl.BlockSpec(memory_space=pl.ANY)
+    hbm = pl.BlockSpec(memory_space=pltpu.HBM)
     return pl.pallas_call(
         fused_kernel,
         out_shape=jax.ShapeDtypeStruct((rows // nh, cols), f32),
@@ -231,14 +247,15 @@
             pltpu.VMEM((Z - 1, rows, chunk), f32),
             pltpu.VMEM((2, rows, chunk), bf16),
             pltpu.VMEM((4, span, rows), f32),
-            pltpu.VMEM((2, chunk // HD, HD, rows), f32),
-            pltpu.VMEM((2, 8, rows), f32),
-            pltpu.VMEM((chunk // HD, HD, rows), f32),
-            pltpu.VMEM((8, rows), f32),
-            pltpu.VMEM((Z, rows, chunk), bf16),
-            pltpu.VMEM((Z, rows, chunk), bf16),
+            pltpu.VMEM((2, per, HD, rows), f32),
+            pltpu.VMEM((2, per, 8, rows), f32),
+            pltpu.VMEM((per, HD, rows), f32),
+            pltpu.VMEM((per, 8, rows), f32),
+            pltpu.VMEM((per, Z, rows, HD), bf16),
+            pltpu.VMEM((per, Z, rows, HD), bf16),
             pltpu.VMEM((rows, cols), f32),
-            pltpu.VMEM((nh - 1, rows // nh, cols), f32),
+            pltpu.VMEM((3, rows // nh, cols), f32),
+            pltpu.VMEM((rows // nh, cols), f32),
             pltpu.SemaphoreType.DMA((4,)),
             pltpu.SemaphoreType.DMA((n_copies,)),
             pltpu.SemaphoreType.DMA((n_copies,)),

time: 103 us -> 91.6 us (0.89)
  Pallas kernels: 96.6 us -> 84.9 us
    pallas_call x1, Pallas kernels: 96.6 us -> 84.9 us  [fused(): pl.pallas_call(fused_kernel, out_shape=jax.ShapeDtypeStruct((rows // nh,...]
where the time goes in v3:
time: 91.6 us; the launch traced here: 91.2 us
  Pallas kernels  84.9 us (93%)
  local copies, waits for them, and re-layouts  6.31 us (7%)
    pallas_call x1, Pallas kernels, fused(): pl.pallas_call(fused_kernel, out_shape=jax.ShapeDtypeStruct((rows // nh,...  84.9 us
    unnamed x13, local copies, waits for them, and re-layouts  6.31 us

profile of v3, /device:TPU:1, one launch (start us, length us, event | category | flops | bytes accessed | tf_op | source)
XLA Modules:
  0.0 91.2 jit_solution(7151913116953681498)
XLA Ops:
  0.0 0.0 copy-start
  0.0 1.2 %copy-done = bf16[8,512,128]{2,1,0:T(8,128)(2,1)S(1)} copy-done((bf16[8,512,128]{2,1,0:T(8,128)(2,1)S(1)}, bf16[8,512,128]{2,1,0:T(8,128)(2,1)}, u32[]{:S(2)}) %copy-start) | copy-done | bytes 1048600
  1.2 0.0 copy-start.1
  1.2 1.2 %copy-done.1 = bf16[8,512,128]{2,1,0:T(8,128)(2,1)S(1)} copy-done((bf16[8,512,128]{2,1,0:T(8,128)(2,1)S(1)}, bf16[8,512,128]{2,1,0:T(8,128)(2,1)}, u32[]{:S(2)}) %copy-start.1) | copy-done | bytes 1048600
  2.5 0.0 copy-start.2
  2.5 1.0 %copy-done.2 = bf16[256,1024]{1,0:T(8,128)(2,1)S(1)} copy-done((bf16[256,1024]{1,0:T(8,128)(2,1)S(1)}, bf16[256,1024]{1,0:T(8,128)(2,1)}, u32[]{:S(2)}) %copy-start.2) | copy-done | bytes 524312
  3.5 0.0 copy-start.3
  3.5 0.8 copy-done.3
  4.3 0.0 copy-start.4
  4.3 0.7 copy-done.4
  4.9 0.0 copy-start.5
  4.9 0.7 copy-done.5
  5.6 84.9 %shard_map.82 = f32[64,1024]{1,0:T(8,128)S(1)} custom-call(bf16[256,1024]{1,0:T(8,128)(2,1)S(1)} %copy-done.2, f32[1,8192]{1,0:T(1,128)S(1)} %bitcast.3, bf16[1024,2048]{1,0:T(8,128)(2,1)} %wq_hbm.1, bf16[8,512,128]{2,1,0:T(8,128)(2,1)S(1)} %copy-done, bf16[8,512,128]{2,1,0:T(8,128)(2,1)S(1)} %copy-done.1, bf16[2048,1024]{1,0:T(8,128)(2,1)} %wo_hbm.1, ...), custom_call_target="tpu_custom_call" | custom-call | tf_op jit(solution)/shard_map/pallas_call | solution.py:230
  90.5 0.7 copy.10
Async XLA Ops:
  0.0 1.2 %copy-start = (bf16[8,512,128]{2,1,0:T(8,128)(2,1)S(1)}, bf16[8,512,128]{2,1,0:T(8,128)(2,1)}, u32[]{:S(2)}) copy-start(bf16[8,512,128]{2,1,0:T(8,128)(2,1)} %k_hbm.1) | copy-start | bytes 3145732
  1.2 1.2 %copy-start.1 = (bf16[8,512,128]{2,1,0:T(8,128)(2,1)S(1)}, bf16[8,512,128]{2,1,0:T(8,128)(2,1)}, u32[]{:S(2)}) copy-start(bf16[8,512,128]{2,1,0:T(8,128)(2,1)} %v_hbm.1) | copy-start | bytes 3145732
  2.5 1.0 %copy-start.2 = (bf16[256,1024]{1,0:T(8,128)(2,1)S(1)}, bf16[256,1024]{1,0:T(8,128)(2,1)}, u32[]{:S(2)}) copy-start(bf16[256,1024]{1,0:T(8,128)(2,1)} %hidden.1) | copy-start | bytes 1572868
  3.5 0.8 copy-start.3
  4.3 0.7 copy-start.4
  4.9 0.7 copy-start.5

commit v4 on v3

--- a/solution.py
+++ b/solution.py
@@ -28,6 +28,7 @@
     rows, feat = hidden.shape
     span = kb.shape[1]
     chunk = qb.shape[2]
+    half = chunk * Z
     out_rows = out.shape[0]
     per_chunk = chunk // HD
     scale = 1.0 / math.sqrt(HD)
@@ -58,7 +59,8 @@
     for k in range(1, nh):
         pl.semaphore_signal(barrier, inc=1, device_id={"head": lax.rem(h + k, nh)}, device_id_type=pl.DeviceIdType.MESH)
 
-    kv_mine = h * X + lax.div(z, X)
+    kv_mine = h * X + x
+    kv_other = h * X + (1 - x)
     locals_ = [
         pltpu.make_async_copy(wq_hbm, wq, local_sem.at[0]),
         pltpu.make_async_copy(k_hbm.at[kv_mine], kb.at[0], local_sem.at[1]),
@@ -79,11 +81,15 @@
     sq[0] = jnp.concatenate(pieces, axis=0)
     pl.semaphore_wait(barrier, nz - 1 + nh - 1)
     sq_copies = [send(sq.at[0], sq.at[k], ctx=lax.rem(c + k, nz)) for k in range(1, nz)]
-    kv_copies = []
-    for k in range(1, Z):
-        idx = h * X + lax.div(zat(k), X)
-        kv_copies.append(send(k_hbm.at[idx], kb.at[k], ctx=at(zat(k), x)))
-        kv_copies.append(send(v_hbm.at[idx], vb.at[k], ctx=at(zat(k), x)))
+    zp = z + 1 - 2 * lax.rem(z, 2)
+
+    def send_kv(idx, slot, zz, xx):
+        return [
+            send(k_hbm.at[idx], kb.at[slot], ctx=at(zz, xx)),
+            send(v_hbm.at[idx], vb.at[slot], ctx=at(zz, xx)),
+        ]
+
+    kv_near = send_kv(kv_mine, 2, zp, x)
     for cp in sq_copies:
         cp.wait_recv()
     total = sq[0]
@@ -97,7 +103,7 @@
         nrm[b * 128 : (b + 1) * 128, :] = (blk * inv_col * g).astype(jnp.bfloat16)
 
     def part(xx, k):
-        cols = pl.ds(pl.multiple_of(at(zat(k), xx) * chunk, chunk), chunk)
+        cols = pl.ds(pl.multiple_of(xx * half + zat(k) * chunk, chunk), chunk)
         return jnp.dot(nrm[...], wq[:, cols], preferred_element_type=f32)
 
     locals_[0].wait()
@@ -105,6 +111,7 @@
     for k in (1, 2, 3, 0):
         xsend[k] = part(1 - x, k)
         x_copies[k] = send(xsend.at[k], xrecv.at[k], ctx=at(z, 1 - x))
+    kv_far = send_kv(kv_other, 1, z, 1 - x) + send_kv(kv_other, 3, zp, 1 - x)
     for k in (1, 2, 3, 0):
         qown[k] = part(x, k)
     z_copies = []
@@ -115,9 +122,9 @@
 
     locals_[1].wait()
     locals_[2].wait()
-    for cp in kv_copies:
+    for cp in kv_near:
         cp.wait_recv()
-    for s in range(Z):
+    for s in (0, 2):
         vt[s] = vb[s].astype(f32).T.astype(jnp.bfloat16)
 
     x_copies[0].wait_recv()
@@ -127,10 +134,15 @@
         qsum = qsum + zrecv[k]
     qb[0] = qsum.astype(jnp.bfloat16)
     beside = at(z, 1 - x)
-    q_copy = send(qb.at[0], qb.at[1], ctx=beside)
+    far = at(zat(2), x)
+    q_copy = send(qb.at[0], qb.at[1], ctx=far)
+    for cp in kv_far:
+        cp.wait_recv()
+    for s in (1, 3):
+        vt[s] = vb[s].astype(f32).T.astype(jnp.bfloat16)
 
     place = lax.broadcasted_iota(jnp.int32, (span, rows), 0)
-    owners = [at(zat(Z - k), x) for k in range(Z)]
+    owners = (at(z, x), at(z, 1 - x), at(zp, x), at(zp, 1 - x))
 
     def attend(i):
         copies = []
@@ -153,8 +165,8 @@
             st[i, j, 0:1, :] = top
             st[i, j, 1:2, :] = tot
             if i == 1:
-                copies.append(send(os_.at[1, j], ocr.at[j], ctx=beside))
-                copies.append(send(st.at[1, j], scr.at[j], ctx=beside))
+                copies.append(send(os_.at[1, j], ocr.at[j], ctx=far))
+                copies.append(send(st.at[1, j], scr.at[j], ctx=far))
         return copies
 
     st[...] = jnp.zeros_like(st)
@@ -176,7 +188,7 @@
         ax_copies[j, 0] = send(az.at[j, 0], ax.at[j, 0], ctx=beside)
 
     def project(piece, xx, j, k):
-        first = pl.multiple_of(at(zat(Z - k), xx) * chunk + j * HD, HD)
+        first = pl.multiple_of(xx * half + zat(Z - k) * chunk + j * HD, HD)
         return jnp.dot(piece, wo[pl.ds(first, HD), :], preferred_element_type=f32)
 
     locals_[3].wait()

time: 91.6 us -> 97.3 us (1.062)
  Pallas kernels: 84.9 us -> 90.7 us
    pallas_call x1, Pallas kernels: 84.9 us -> 90.7 us  [fused(): pl.pallas_call(fused_kernel, out_shape=jax.ShapeDtypeStruct((rows // nh,...]
where the time goes in v4:
time: 97.3 us; the launch traced here: 97 us
  Pallas kernels  90.7 us (93%)
  local copies, waits for them, and re-layouts  6.31 us (6%)
    pallas_call x1, Pallas kernels, fused(): pl.pallas_call(fused_kernel, out_shape=jax.ShapeDtypeStruct((rows // nh,...  90.7 us
    unnamed x13, local copies, waits for them, and re-layouts  6.31 us

profile of v4, /device:TPU:1, one launch (start us, length us, event | category | flops | bytes accessed | tf_op | source)
XLA Modules:
  0.0 97.0 jit_solution(11268033662006592119)
XLA Ops:
  0.0 0.0 copy-start
  0.0 1.2 %copy-done = bf16[8,512,128]{2,1,0:T(8,128)(2,1)S(1)} copy-done((bf16[8,512,128]{2,1,0:T(8,128)(2,1)S(1)}, bf16[8,512,128]{2,1,0:T(8,128)(2,1)}, u32[]{:S(2)}) %copy-start) | copy-done | bytes 1048600
  1.2 0.0 copy-start.1
  1.2 1.2 %copy-done.1 = bf16[8,512,128]{2,1,0:T(8,128)(2,1)S(1)} copy-done((bf16[8,512,128]{2,1,0:T(8,128)(2,1)S(1)}, bf16[8,512,128]{2,1,0:T(8,128)(2,1)}, u32[]{:S(2)}) %copy-start.1) | copy-done | bytes 1048600
  2.5 0.0 copy-start.2
  2.5 1.0 %copy-done.2 = bf16[256,1024]{1,0:T(8,128)(2,1)S(1)} copy-done((bf16[256,1024]{1,0:T(8,128)(2,1)S(1)}, bf16[256,1024]{1,0:T(8,128)(2,1)}, u32[]{:S(2)}) %copy-start.2) | copy-done | bytes 524312
  3.5 0.0 copy-start.3
  3.5 0.8 copy-done.3
  4.3 0.0 copy-start.4
  4.3 0.7 copy-done.4
  4.9 0.0 copy-start.5
  4.9 0.7 copy-done.5
  5.6 90.7 %shard_map.82 = f32[64,1024]{1,0:T(8,128)S(1)} custom-call(bf16[256,1024]{1,0:T(8,128)(2,1)S(1)} %copy-done.2, f32[1,8192]{1,0:T(1,128)S(1)} %bitcast.3, bf16[1024,2048]{1,0:T(8,128)(2,1)} %wq_hbm.1, bf16[8,512,128]{2,1,0:T(8,128)(2,1)S(1)} %copy-done, bf16[8,512,128]{2,1,0:T(8,128)(2,1)S(1)} %copy-done.1, bf16[2048,1024]{1,0:T(8,128)(2,1)} %wo_hbm.1, ...), custom_call_target="tpu_custom_call" | custom-call | tf_op jit(solution)/shard_map/pallas_call | solution.py:242
  96.3 0.7 copy.10
Async XLA Ops:
  0.0 1.2 %copy-start = (bf16[8,512,128]{2,1,0:T(8,128)(2,1)S(1)}, bf16[8,512,128]{2,1,0:T(8,128)(2,1)}, u32[]{:S(2)}) copy-start(bf16[8,512,128]{2,1,0:T(8,128)(2,1)} %k_hbm.1) | copy-start | bytes 3145732
  1.2 1.2 %copy-start.1 = (bf16[8,512,128]{2,1,0:T(8,128)(2,1)S(1)}, bf16[8,512,128]{2,1,0:T(8,128)(2,1)}, u32[]{:S(2)}) copy-start(bf16[8,512,128]{2,1,0:T(8,128)(2,1)} %v_hbm.1) | copy-start | bytes 3145732
  2.5 1.0 %copy-start.2 = (bf16[256,1024]{1,0:T(8,128)(2,1)S(1)}, bf16[256,1024]{1,0:T(8,128)(2,1)}, u32[]{:S(2)}) copy-start(bf16[256,1024]{1,0:T(8,128)(2,1)} %hidden.1) | copy-start | bytes 1572868
  3.5 0.8 copy-start.3
  4.3 0.7 copy-start.4
  4.9 0.7 copy-start.5
